TPU v7x, 128 devices: a whole 4x4x4 slice. The times are simulated.
128 devices in a mesh: seq: 16 (over y, z_lo, core), vis: 8 (over z_hi, x).
Axes of the slice: x: 4, y: 4, z: 4 (z_hi: 2, z_lo: 2; z = z_hi * 2 + z_lo), core: 2. Of those that a mesh axis runs over, the one named last changes fastest.
Arguments:
- text: bfloat16 [4096, 8192], P('seq'), may hold values from -6 to 6
- frames: bfloat16 [4096, 8192], P(('seq', 'vis')), may hold values from -60 to 60
- tile_pos: int32 [4096], P(('seq', 'vis')), may hold values from 0 to 4095, as said below
- frame_count: int32 [128], P(('seq', 'vis')), may hold values from 2 to 32
- doc_ids: int32 [4096], replicated, may hold values from 0 to 3, never falling along the last dimension, each value on 1 to 2048 neighbouring positions
- norm_gain: float32 [8192], replicated, may hold values from 0.1 to 1.9
- w_query: bfloat16 [8192, 8192], P(None, 'vis'), may hold values from -4 to 4
- q_bias: float32 [8192], P('vis'), may hold values from -3 to 3
- w_key: bfloat16 [8192, 1024], P(None, 'vis'), may hold values from -4 to 4
- w_value: bfloat16 [8192, 1024], P(None, 'vis'), may hold values from -0.0625 to 0.0625
- v_bias: float32 [1024], P('vis'), may hold values from -3 to 3
Outputs:
- attended: bfloat16 [4096, 8192], P('seq', 'vis')
Inputs may be any that keep to these rules, and one draw needn't show every extreme that they name: `tile_pos`: all entries together name every position of the window once. Of one device's 32 rows, at most 2 of those below its frame_count fall into one shard of 256 positions, and in every draw one shard receives exactly 2 usable rows from every device. Rows at or beyond the count are unused. `doc_ids`: never falling along the window.
All inputs are finite; a program needn't handle non-finite values.
Results may differ from a plain program's by a relative error of at most 0.0069.
Values may be sent and summed in bfloat16 or wider, within the bound.
A program may use at most 128 MiB of HBM per device.

v0:
```python
import jax
import jax.numpy as jnp
from jax import lax
from jax.sharding import PartitionSpec as P

HEAD_DIM = 128
epsilon = 1e-06
negative = -1e30


def frame_slots(frames, tile_pos, frame_count, shard_rows, owners, capacity):
    row_count = frames.shape[0]
    row_ids = jnp.arange(row_count, dtype=jnp.int32)
    usable = row_ids < frame_count[0]
    owner = jnp.where(usable, tile_pos // shard_rows, owners)
    hits = (owner[:, None] == jnp.arange(owners, dtype=jnp.int32)[None, :]).astype(jnp.int32)
    earlier = (row_ids[:, None] > row_ids[None, :]).astype(jnp.int32)
    before = jnp.dot(earlier, hits, preferred_element_type=jnp.int32)
    rank = jnp.sum(before * hits, axis=1)
    slot_index = owner * capacity + rank
    slot_ids = jnp.arange(owners * capacity, dtype=jnp.int32)
    match = usable[:, None] & (slot_index[:, None] == slot_ids[None, :])
    filled = jnp.any(match, axis=0)
    source = jnp.sum(jnp.where(match, row_ids[:, None], 0), axis=0)
    slot_rows = jnp.where(filled[:, None], frames[source], jnp.zeros((), frames.dtype))
    slot_place = jnp.where(filled, tile_pos[source], -1)
    return (
        slot_rows.reshape(owners, capacity, frames.shape[1]),
        slot_place.reshape(owners, capacity),
    )


def place_frames(text, incoming, incoming_place, first_row):
    local_place = incoming_place - first_row
    lookup = local_place[None, :] == jnp.arange(text.shape[0], dtype=jnp.int32)[:, None]
    covered = jnp.any(lookup, axis=1)
    source = jnp.sum(
        jnp.where(lookup, jnp.arange(local_place.shape[0], dtype=jnp.int32)[None, :], 0), axis=1
    )
    return jnp.where(covered[:, None], incoming[source], text)


def attend_block(
    block_state, query_rows, query_place, query_docs, key_block, key_place, key_docs, kv_heads
):
    row_peak, row_total, summed = block_state
    row_count = query_rows.shape[0]
    grouped = query_rows.reshape(row_count, kv_heads, -1, HEAD_DIM)
    key_width = kv_heads * HEAD_DIM
    key_part = key_block[:, :key_width].reshape(-1, kv_heads, HEAD_DIM)
    value_part = key_block[:, key_width:].reshape(-1, kv_heads, HEAD_DIM)
    scores = jnp.einsum(
        "qgjd,kgd->qgjk", grouped, key_part, preferred_element_type=jnp.float32
    ) * HEAD_DIM ** (-0.5)
    allowed = (key_place[None, :] <= query_place[:, None]) & (
        key_docs[None, :] == query_docs[:, None]
    )
    allowed = allowed[:, None, None, :]
    block_peak = jnp.max(jnp.where(allowed, scores, negative), axis=3)
    new_peak = jnp.maximum(row_peak, block_peak)
    raised = jnp.where(allowed, jnp.exp(scores - new_peak[..., None]), 0.0)
    factor = jnp.exp(row_peak - new_peak)
    new_total = row_total * factor + jnp.sum(raised, axis=3)
    product = jnp.einsum(
        "qgjk,kgd->qgjd",
        raised.astype(jnp.bfloat16),
        value_part,
        preferred_element_type=jnp.float32,
    )
    return (new_peak, new_total, summed * factor[..., None] + product)


def on_device(
    text, frames, tile_pos, frame_count, doc_ids, norm_gain, w_query, q_bias, w_key, w_value, v_bias
):
    seq_count = lax.axis_size("seq")
    vis_count = lax.axis_size("vis")
    shard_index = lax.axis_index("seq")
    shard_rows = text.shape[0]
    capacity = shard_rows // (seq_count * vis_count)
    first_row = shard_index * shard_rows
    slot_rows, slot_place = frame_slots(
        frames, tile_pos, frame_count, shard_rows, seq_count, capacity
    )
    wide_rows = jnp.broadcast_to(slot_rows[:, None], (seq_count, vis_count) + slot_rows.shape[1:])
    wide_rows = wide_rows.reshape(seq_count * vis_count, capacity, slot_rows.shape[2])
    wide_place = jnp.broadcast_to(slot_place[:, None], (seq_count, vis_count, capacity))
    wide_place = wide_place.reshape(seq_count * vis_count, capacity)
    incoming, incoming_place = (
        lax.all_to_all(wide_rows, ("seq", "vis"), split_axis=0, concat_axis=0, tiled=True),
        lax.all_to_all(wide_place, ("seq", "vis"), split_axis=0, concat_axis=0, tiled=True),
    )
    incoming = incoming.reshape(-1, incoming.shape[-1])
    incoming_place = incoming_place.reshape(-1)
    merged = place_frames(text, incoming, incoming_place, first_row)
    widened = merged.astype(jnp.float32)
    mean_square = jnp.mean(widened * widened, axis=1, keepdims=True)
    normed = (widened * lax.rsqrt(mean_square + epsilon) * norm_gain).astype(jnp.bfloat16)
    queries = (jnp.dot(normed, w_query, preferred_element_type=jnp.float32) + q_bias).astype(
        jnp.bfloat16
    )
    key_rows = jnp.dot(normed, w_key, preferred_element_type=jnp.float32).astype(jnp.bfloat16)
    value_rows = (jnp.dot(normed, w_value, preferred_element_type=jnp.float32) + v_bias).astype(
        jnp.bfloat16
    )
    keyval = jnp.concatenate([key_rows, value_rows], axis=1)
    kv_heads = w_key.shape[1] // HEAD_DIM
    per_group = w_query.shape[1] // HEAD_DIM // kv_heads
    own_place = first_row + jnp.arange(shard_rows, dtype=jnp.int32)
    own_docs = lax.dynamic_slice_in_dim(doc_ids, first_row, shard_rows)
    blocks = [(queries, own_place, own_docs)]
    initial = tuple(
        (
            (
                jnp.full((entry[0].shape[0], kv_heads, per_group), negative, jnp.float32),
                jnp.zeros((entry[0].shape[0], kv_heads, per_group), jnp.float32),
                jnp.zeros((entry[0].shape[0], kv_heads, per_group, HEAD_DIM), jnp.float32),
            )
            for entry in blocks
        )
    )
    incoming_keys = lax.all_gather(keyval, "seq", axis=0, tiled=True)
    piece_rows = incoming_keys.shape[0]
    step_rows = 512

    def one_step(step_index, current):
        key_first = step_index * step_rows
        key_block = lax.dynamic_slice_in_dim(incoming_keys, step_index * step_rows, step_rows)
        key_place = key_first + jnp.arange(step_rows, dtype=jnp.int32)
        key_docs = lax.dynamic_slice_in_dim(doc_ids, key_first, step_rows)
        updated = []
        for entry, block_state in zip(blocks, current):
            query_rows, query_place, query_docs = entry

            def compute(
                operand, query_rows=query_rows, query_place=query_place, query_docs=query_docs
            ):
                return attend_block(
                    operand,
                    query_rows,
                    query_place,
                    query_docs,
                    key_block,
                    key_place,
                    key_docs,
                    kv_heads,
                )

            def unchanged(operand):
                return operand

            updated.append(lax.cond(key_first <= query_place[-1], compute, unchanged, block_state))
        return tuple(updated)

    finals = lax.fori_loop(0, piece_rows // step_rows, one_step, initial)
    outputs = [
        (summed / row_total[..., None]).reshape(summed.shape[0], -1).astype(jnp.bfloat16)
        for row_peak, row_total, summed in finals
    ]
    return outputs[0]


def solution(mesh):
    in_specs = (
        P("seq", None),
        P(("seq", "vis"), None),
        P(("seq", "vis")),
        P(("seq", "vis")),
        P(),
        P(),
        P(None, "vis"),
        P("vis"),
        P(None, "vis"),
        P(None, "vis"),
        P("vis"),
    )
    out_specs = P("seq", "vis")
    return jax.shard_map(
        on_device, mesh=mesh, in_specs=in_specs, out_specs=out_specs, check_vma=False
    )
```

profile of v0, /device:TPU:57, one launch (start us, length us, event | category | flops | bytes accessed | tf_op | source)
XLA Modules:
  0.0 259.8 jit_solution(562289550122915700)
XLA Ops:
  11.2 10.4 %all-to-all-start = ((s32[128,1,2]{2,1,0:T(1,128)}), s32[128,1,2]{2,1,0:T(1,128)S(1)}, u32[]{:S(2)}, u32[]{:S(2)}) async-start(s32[128,1,2]{2,1,0:T(1,128)} %bitcast.16), calls=%async_computation | async-start | bytes 131072 | tf_op jit(solution)/shard_map/all_to_all | solution.py:91
  28.7 6.1 %broadcast_in_dim.133 = bf16[16,8,2,8192]{3,2,1,0:T(2,128)(2,1)} broadcast(bf16[16,2,8192]{2,1,0:T(2,128)(2,1)S(1)} %broadcast_select_fusion.1), dimensions={0,2,3} | broadcast | bytes 4718592 | tf_op jit(solution)/shard_map/broadcast_in_dim | solution.py:85
  34.8 8.2 %all-to-all-start.1 = ((bf16[128,2,8192]{2,1,0:T(2,128)(2,1)}), bf16[128,2,8192]{2,1,0:T(2,128)(2,1)}, u32[]{:S(2)}, u32[]{:S(2)}) async-start(bf16[128,2,8192]{2,1,0:T(2,128)(2,1)} %bitcast.83), calls=%async_computation.1 | async-start | bytes 8388608 | tf_op jit(solution)/shard_map/all_to_all | solution.py:90
  43.6 48.8 %all-to-all-done.1 = bf16[128,2,8192]{2,1,0:T(2,128)(2,1)} async-done(((bf16[128,2,8192]{2,1,0:T(2,128)(2,1)}), bf16[128,2,8192]{2,1,0:T(2,128)(2,1)}, u32[]{:S(2)}, u32[]{:S(2)}) %all-to-all-start.1) | async-done | bytes 4194336 | tf_op jit(solution)/shard_map/all_to_all | solution.py:90
  92.5 7.2 %reshape.191 = bf16[256,8192]{1,0:T(8,128)(2,1)} reshape(bf16[128,2,8192]{2,1,0:T(2,128)(2,1)} %all-to-all-done.1) | data formatting | bytes 8388608 | tf_op jit(solution)/shard_map/reshape | solution.py:93
  99.7 11.7 %gather_fusion.2 = bf16[256,8192]{1,0:T(8,128)(2,1)} fusion(bf16[256,8192]{1,0:T(8,128)(2,1)} %reshape.191, s32[1024]{0:T(1024)S(1)} %pad_clamp_fusion), kind=kCustom, calls=%fused_computation.2 | custom fusion | bytes 8389632 | tf_op jit(solution)/shard_map/gather | solution.py:40
  111.3 5.1 %fusion.22 = f32[256]{0:T(256)S(1)} fusion(bf16[256,8192]{1,0:T(8,128)(2,1)} %gather_fusion.2, bf16[256,8192]{1,0:T(8,128)(2,1)} %param.15, pred[256]{0:T(512)(128)(4,1)S(1)} %fusion.28), kind=kLoop, calls=%fused_computation.31 | loop fusion | flops 8388352 | bytes 8389888 | tf_op jit(solution)/shard_map/reduce_sum | solution.py:97
  126.2 12.3 %fusion.25 = bf16[256,1024]{1,0:T(8,128)(2,1)} fusion(bf16[256,8192]{1,0:T(8,128)(2,1)} %copy-done.2, bf16[8192,1024]{1,0:T(8,128)(2,1)} %param.21, f32[1024]{0:T(1024)S(1)} %copy-done.8), kind=kOutput, calls=%fused_computation.36 | convolution fusion | flops 4295491584 | bytes 21499904 | tf_op jit(solution)/shard_map/dot_general | solution.py:99
  138.5 22.6 %all-gather.2.cloned.1.call-done = bf16[4096,256]{0,1:T(8,128)(2,1)} async-done(((bf16[256,256]{0,1:T(8,128)(2,1)}), bf16[4096,256]{0,1:T(8,128)(2,1)}) %all-gather.2.cloned.1.call-update) | async-done | bytes 2097168 | tf_op jit(solution)/shard_map/all_gather | solution.py:122
  161.1 4.1 %copy.30 = bf16[4096,256]{1,0:T(8,128)(2,1)} copy(bf16[4096,256]{0,1:T(8,128)(2,1)} %all-gather.2.cloned.1.call-done) | data formatting | bytes 4194304 | tf_op jit(solution)/shard_map/while | solution.py:155
  165.3 84.8 %while.17 = (s32[]{:T(128)}, f32[256,1,8]{0,2,1:T(8,128)S(1)}, f32[256,1,8]{0,2,1:T(8,128)S(1)}, f32[256,1,8,128]{0,3,2,1:T(8,128)S(1)}, s32[256]{0:T(256)S(1)},...) while((s32[]{:T(128)}, f32[256,1,8]{0,2,1:T(8,128)S(1)}, ...), condition=%wide.region_11.12_spmd, body=%wide.region_6.11_spmd.sunk | while | flops 549329408 | bytes 32915828 | solution.py:155
  166.6 9.3 %conditional.2 = ((f32[256,1,8]{0,2,1:T(8,128)S(1)}, f32[256,1,8]{0,2,1:T(8,128)S(1)}, f32[256,1,8,128]{0,3,2,1:T(8,128)S(1)})) conditional(s32[]{:T(128)} %convert_element_type.65, (f32[256,1,8]{0,2,1:T(8,128)S(1)}, f32[256,1,8]{0,2,1:T(8,128)S(1)}, f32[256,1,8,128]{0,3,2,1:T(8,128)S(1)}) %tuple.52, (s32[]{:T(128)}, s32[512]{0:T(512)S(1)}, ...), branch_computations={%region_7.7_spmd, %region_8.10_spmd} | conditional | flops 549329408 | bytes 32913534 | solution.py:152
  167.6 3.8 %fusion = (f32[256,8]{0,1:T(8,128)S(1)}, f32[512,256,8]{1,0,2:T(8,128)}) fusion(pred[256,512]{0,1:T(8,128)(4,1)S(1)} %compare_and_fusion, bf16[4096,256]{1,0:T(8,128)(2,1)} %get-tuple-element.272, s32[]{:T(128)S(6)} %select_n.70, bf16[256,1024]{1,0:T(8,128)(2,1)} %get-tuple-element.273), kind=kOutput, calls=%fused_computation.5 | convolution fusion | flops 271579136 | bytes 4988932 | tf_op jit(solution)/shard_map/while/body/eval_jaxpr/cond/branch_1_fun/qgjd,kgd->qgjk/dot_general | solution.py:52
  177.2 9.3 %conditional.2 = ((f32[256,1,8]{0,2,1:T(8,128)S(1)}, f32[256,1,8]{0,2,1:T(8,128)S(1)}, f32[256,1,8,128]{0,3,2,1:T(8,128)S(1)})) conditional(s32[]{:T(128)} %convert_element_type.65, (f32[256,1,8]{0,2,1:T(8,128)S(1)}, f32[256,1,8]{0,2,1:T(8,128)S(1)}, f32[256,1,8,128]{0,3,2,1:T(8,128)S(1)}) %tuple.52, (s32[]{:T(128)}, s32[512]{0:T(512)S(1)}, ...), branch_computations={%region_7.7_spmd, %region_8.10_spmd} | conditional | flops 549329408 | bytes 32913534 | solution.py:152
  178.2 3.8 %fusion = (f32[256,8]{0,1:T(8,128)S(1)}, f32[512,256,8]{1,0,2:T(8,128)}) fusion(pred[256,512]{0,1:T(8,128)(4,1)S(1)} %compare_and_fusion, bf16[4096,256]{1,0:T(8,128)(2,1)} %get-tuple-element.272, s32[]{:T(128)S(6)} %select_n.70, bf16[256,1024]{1,0:T(8,128)(2,1)} %get-tuple-element.273), kind=kOutput, calls=%fused_computation.5 | convolution fusion | flops 271579136 | bytes 4988932 | tf_op jit(solution)/shard_map/while/body/eval_jaxpr/cond/branch_1_fun/qgjd,kgd->qgjk/dot_general | solution.py:52
  187.7 9.3 %conditional.2 = ((f32[256,1,8]{0,2,1:T(8,128)S(1)}, f32[256,1,8]{0,2,1:T(8,128)S(1)}, f32[256,1,8,128]{0,3,2,1:T(8,128)S(1)})) conditional(s32[]{:T(128)} %convert_element_type.65, (f32[256,1,8]{0,2,1:T(8,128)S(1)}, f32[256,1,8]{0,2,1:T(8,128)S(1)}, f32[256,1,8,128]{0,3,2,1:T(8,128)S(1)}) %tuple.52, (s32[]{:T(128)}, s32[512]{0:T(512)S(1)}, ...), branch_computations={%region_7.7_spmd, %region_8.10_spmd} | conditional | flops 549329408 | bytes 32913534 | solution.py:152
  188.8 3.8 %fusion = (f32[256,8]{0,1:T(8,128)S(1)}, f32[512,256,8]{1,0,2:T(8,128)}) fusion(pred[256,512]{0,1:T(8,128)(4,1)S(1)} %compare_and_fusion, bf16[4096,256]{1,0:T(8,128)(2,1)} %get-tuple-element.272, s32[]{:T(128)S(6)} %select_n.70, bf16[256,1024]{1,0:T(8,128)(2,1)} %get-tuple-element.273), kind=kOutput, calls=%fused_computation.5 | convolution fusion | flops 271579136 | bytes 4988932 | tf_op jit(solution)/shard_map/while/body/eval_jaxpr/cond/branch_1_fun/qgjd,kgd->qgjk/dot_general | solution.py:52
  198.3 9.3 %conditional.2 = ((f32[256,1,8]{0,2,1:T(8,128)S(1)}, f32[256,1,8]{0,2,1:T(8,128)S(1)}, f32[256,1,8,128]{0,3,2,1:T(8,128)S(1)})) conditional(s32[]{:T(128)} %convert_element_type.65, (f32[256,1,8]{0,2,1:T(8,128)S(1)}, f32[256,1,8]{0,2,1:T(8,128)S(1)}, f32[256,1,8,128]{0,3,2,1:T(8,128)S(1)}) %tuple.52, (s32[]{:T(128)}, s32[512]{0:T(512)S(1)}, ...), branch_computations={%region_7.7_spmd, %region_8.10_spmd} | conditional | flops 549329408 | bytes 32913534 | solution.py:152
  199.3 3.8 %fusion = (f32[256,8]{0,1:T(8,128)S(1)}, f32[512,256,8]{1,0,2:T(8,128)}) fusion(pred[256,512]{0,1:T(8,128)(4,1)S(1)} %compare_and_fusion, bf16[4096,256]{1,0:T(8,128)(2,1)} %get-tuple-element.272, s32[]{:T(128)S(6)} %select_n.70, bf16[256,1024]{1,0:T(8,128)(2,1)} %get-tuple-element.273), kind=kOutput, calls=%fused_computation.5 | convolution fusion | flops 271579136 | bytes 4988932 | tf_op jit(solution)/shard_map/while/body/eval_jaxpr/cond/branch_1_fun/qgjd,kgd->qgjk/dot_general | solution.py:52
  208.9 9.3 %conditional.2 = ((f32[256,1,8]{0,2,1:T(8,128)S(1)}, f32[256,1,8]{0,2,1:T(8,128)S(1)}, f32[256,1,8,128]{0,3,2,1:T(8,128)S(1)})) conditional(s32[]{:T(128)} %convert_element_type.65, (f32[256,1,8]{0,2,1:T(8,128)S(1)}, f32[256,1,8]{0,2,1:T(8,128)S(1)}, f32[256,1,8,128]{0,3,2,1:T(8,128)S(1)}) %tuple.52, (s32[]{:T(128)}, s32[512]{0:T(512)S(1)}, ...), branch_computations={%region_7.7_spmd, %region_8.10_spmd} | conditional | flops 549329408 | bytes 32913534 | solution.py:152
  209.9 3.8 %fusion = (f32[256,8]{0,1:T(8,128)S(1)}, f32[512,256,8]{1,0,2:T(8,128)}) fusion(pred[256,512]{0,1:T(8,128)(4,1)S(1)} %compare_and_fusion, bf16[4096,256]{1,0:T(8,128)(2,1)} %get-tuple-element.272, s32[]{:T(128)S(6)} %select_n.70, bf16[256,1024]{1,0:T(8,128)(2,1)} %get-tuple-element.273), kind=kOutput, calls=%fused_computation.5 | convolution fusion | flops 271579136 | bytes 4988932 | tf_op jit(solution)/shard_map/while/body/eval_jaxpr/cond/branch_1_fun/qgjd,kgd->qgjk/dot_general | solution.py:52
  219.5 9.3 %conditional.2 = ((f32[256,1,8]{0,2,1:T(8,128)S(1)}, f32[256,1,8]{0,2,1:T(8,128)S(1)}, f32[256,1,8,128]{0,3,2,1:T(8,128)S(1)})) conditional(s32[]{:T(128)} %convert_element_type.65, (f32[256,1,8]{0,2,1:T(8,128)S(1)}, f32[256,1,8]{0,2,1:T(8,128)S(1)}, f32[256,1,8,128]{0,3,2,1:T(8,128)S(1)}) %tuple.52, (s32[]{:T(128)}, s32[512]{0:T(512)S(1)}, ...), branch_computations={%region_7.7_spmd, %region_8.10_spmd} | conditional | flops 549329408 | bytes 32913534 | solution.py:152
  230.1 9.3 %conditional.2 = ((f32[256,1,8]{0,2,1:T(8,128)S(1)}, f32[256,1,8]{0,2,1:T(8,128)S(1)}, f32[256,1,8,128]{0,3,2,1:T(8,128)S(1)})) conditional(s32[]{:T(128)} %convert_element_type.65, (f32[256,1,8]{0,2,1:T(8,128)S(1)}, f32[256,1,8]{0,2,1:T(8,128)S(1)}, f32[256,1,8,128]{0,3,2,1:T(8,128)S(1)}) %tuple.52, (s32[]{:T(128)}, s32[512]{0:T(512)S(1)}, ...), branch_computations={%region_7.7_spmd, %region_8.10_spmd} | conditional | flops 549329408 | bytes 32913534 | solution.py:152
  240.7 9.3 %conditional.2 = ((f32[256,1,8]{0,2,1:T(8,128)S(1)}, f32[256,1,8]{0,2,1:T(8,128)S(1)}, f32[256,1,8,128]{0,3,2,1:T(8,128)S(1)})) conditional(s32[]{:T(128)} %convert_element_type.65, (f32[256,1,8]{0,2,1:T(8,128)S(1)}, f32[256,1,8]{0,2,1:T(8,128)S(1)}, f32[256,1,8,128]{0,3,2,1:T(8,128)S(1)}) %tuple.52, (s32[]{:T(128)}, s32[512]{0:T(512)S(1)}, ...), branch_computations={%region_7.7_spmd, %region_8.10_spmd} | conditional | flops 549329408 | bytes 32913534 | solution.py:152
  (152 shorter events, 83.8 us)
Async XLA Ops:
  6.5 113.5 %copy-start = (bf16[8192,128]{1,0:T(8,128)(2,1)S(1)}, bf16[8192,128]{1,0:T(8,128)(2,1)}, u32[]{:S(2)}) copy-start(bf16[8192,128]{1,0:T(8,128)(2,1)} %param.23) | copy-start | bytes 6291460
  11.2 17.4 %all-to-all-start = ((s32[128,1,2]{2,1,0:T(1,128)}), s32[128,1,2]{2,1,0:T(1,128)S(1)}, u32[]{:S(2)}, u32[]{:S(2)}) async-start(s32[128,1,2]{2,1,0:T(1,128)} %bitcast.16), calls=%async_computation | async-start | bytes 131072 | tf_op jit(solution)/shard_map/all_to_all | solution.py:91
  34.8 57.7 %all-to-all-start.1 = ((bf16[128,2,8192]{2,1,0:T(2,128)(2,1)}), bf16[128,2,8192]{2,1,0:T(2,128)(2,1)}, u32[]{:S(2)}, u32[]{:S(2)}) async-start(bf16[128,2,8192]{2,1,0:T(2,128)(2,1)} %bitcast.83), calls=%async_computation.1 | async-start | bytes 8388608 | tf_op jit(solution)/shard_map/all_to_all | solution.py:90
  43.0 118.1 %all-gather.2.cloned.1.call-start = ((), (), s32[]{:S(2)}) async-start(), calls=%async_computation.2 | async-start | bytes 2228224 | tf_op jit(solution)/shard_map/all_gather | solution.py:122
  99.7 16.8 %copy-start.6 = (f32[8192]{0:T(1024)S(1)}, f32[8192]{0:T(1024)}, u32[]{:S(2)}) copy-start(f32[8192]{0:T(1024)} %param.20) | copy-start | bytes 98308
  111.3 5.2 %copy-start.3 = (bf16[256,8192]{1,0:T(8,128)(2,1)S(1)}, bf16[256,8192]{1,0:T(8,128)(2,1)}, u32[]{:S(2)}) copy-start(bf16[256,8192]{1,0:T(8,128)(2,1)} %gather_fusion.2) | copy-start | bytes 12582916
  111.3 5.9 %copy-start.4 = (bf16[256,8192]{1,0:T(8,128)(2,1)S(1)}, bf16[256,8192]{1,0:T(8,128)(2,1)}, u32[]{:S(2)}) copy-start(bf16[256,8192]{1,0:T(8,128)(2,1)} %param.15) | copy-start | bytes 12582916
  120.1 4.7 %copy-start.2 = (bf16[256,8192]{1,0:T(8,128)(2,1)}, bf16[256,8192]{1,0:T(8,128)(2,1)S(1)}, u32[]{:S(2)}) copy-start(bf16[256,8192]{1,0:T(8,128)(2,1)S(1)} %fusion.24) | copy-start | bytes 12582916
  120.1 3.1 %copy-start.5 = (bf16[8192,128]{1,0:T(8,128)(2,1)S(1)}, bf16[8192,128]{1,0:T(8,128)(2,1)}, u32[]{:S(2)}) copy-start(bf16[8192,128]{1,0:T(8,128)(2,1)} %param.24) | copy-start | bytes 6291460
  120.1 3.1 %copy-start.7 = (f32[128]{0:T(128)S(1)}, f32[128]{0:T(128)}, u32[]{:S(2)}) copy-start(f32[128]{0:T(128)} %param.25) | copy-start | bytes 1540
  123.2 3.0 %copy-start.8 = (f32[1024]{0:T(1024)S(1)}, f32[1024]{0:T(1024)}, u32[]{:S(2)}) copy-start(f32[1024]{0:T(1024)} %param.22) | copy-start | bytes 12292
  171.4 3.6 %copy-start.1 = (f32[512,256,8]{1,0,2:T(8,128)S(1)}, f32[512,256,8]{1,0,2:T(8,128)}, u32[]{:S(2)}) copy-start(f32[512,256,8]{1,0,2:T(8,128)} %get-tuple-element.350) | copy-start | bytes 12582916 | tf_op jit(solution)/shard_map/while/body/eval_jaxpr/cond
  182.0 3.6 %copy-start.1 = (f32[512,256,8]{1,0,2:T(8,128)S(1)}, f32[512,256,8]{1,0,2:T(8,128)}, u32[]{:S(2)}) copy-start(f32[512,256,8]{1,0,2:T(8,128)} %get-tuple-element.350) | copy-start | bytes 12582916 | tf_op jit(solution)/shard_map/while/body/eval_jaxpr/cond
  192.6 3.6 %copy-start.1 = (f32[512,256,8]{1,0,2:T(8,128)S(1)}, f32[512,256,8]{1,0,2:T(8,128)}, u32[]{:S(2)}) copy-start(f32[512,256,8]{1,0,2:T(8,128)} %get-tuple-element.350) | copy-start | bytes 12582916 | tf_op jit(solution)/shard_map/while/body/eval_jaxpr/cond
  203.2 3.6 %copy-start.1 = (f32[512,256,8]{1,0,2:T(8,128)S(1)}, f32[512,256,8]{1,0,2:T(8,128)}, u32[]{:S(2)}) copy-start(f32[512,256,8]{1,0,2:T(8,128)} %get-tuple-element.350) | copy-start | bytes 12582916 | tf_op jit(solution)/shard_map/while/body/eval_jaxpr/cond
  213.8 3.6 %copy-start.1 = (f32[512,256,8]{1,0,2:T(8,128)S(1)}, f32[512,256,8]{1,0,2:T(8,128)}, u32[]{:S(2)}) copy-start(f32[512,256,8]{1,0,2:T(8,128)} %get-tuple-element.350) | copy-start | bytes 12582916 | tf_op jit(solution)/shard_map/while/body/eval_jaxpr/cond
  224.4 3.6 %copy-start.1 = (f32[512,256,8]{1,0,2:T(8,128)S(1)}, f32[512,256,8]{1,0,2:T(8,128)}, u32[]{:S(2)}) copy-start(f32[512,256,8]{1,0,2:T(8,128)} %get-tuple-element.350) | copy-start | bytes 12582916 | tf_op jit(solution)/shard_map/while/body/eval_jaxpr/cond
  235.0 3.6 %copy-start.1 = (f32[512,256,8]{1,0,2:T(8,128)S(1)}, f32[512,256,8]{1,0,2:T(8,128)}, u32[]{:S(2)}) copy-start(f32[512,256,8]{1,0,2:T(8,128)} %get-tuple-element.350) | copy-start | bytes 12582916 | tf_op jit(solution)/shard_map/while/body/eval_jaxpr/cond
  245.5 3.6 %copy-start.1 = (f32[512,256,8]{1,0,2:T(8,128)S(1)}, f32[512,256,8]{1,0,2:T(8,128)}, u32[]{:S(2)}) copy-start(f32[512,256,8]{1,0,2:T(8,128)} %get-tuple-element.350) | copy-start | bytes 12582916 | tf_op jit(solution)/shard_map/while/body/eval_jaxpr/cond
Sparse Core Ops, SparseCore 0:
  125.5 35.5 all-gather.1
where the time goes:
time: 261 us; the launch traced here: 260 us
  waiting for transfers between devices  75.1 us (29%)
  matrix products  74.8 us (29%)
  local copies, waits for them, and re-layouts  50.3 us (19%)
  other arithmetic  20.7 us (8%)
  starting transfers between devices  18.6 us (7%)
  between operations  14.4 us (6%)
  loops' own time  5.92 us (2%)
    all_to_all x1, waiting for transfers between devices, on_device(): lax.all_to_all(wide_rows, ('seq', 'vis'), split_axis=0, concat_axis=0, ti...  48.8 us
    dot_general x8, matrix products, attend_block(): jnp.einsum('qgjd,kgd->qgjk', grouped, key_part, preferred_element_type=jn...  30.6 us
    dot_general x8, matrix products, attend_block(): jnp.einsum('qgjk,kgd->qgjd', raised.astype(jnp.bfloat16), value_part, pre...  28.5 us
    all_gather x1, waiting for transfers between devices, on_device(): incoming_keys = lax.all_gather(keyval, 'seq', axis=0, tiled=True)  22.6 us
    dot_general x1, matrix products, on_device(): jnp.dot(normed, w_query, preferred_element_type=jnp.float32) + q_bias  12.3 us
    gather x1, local copies, waits for them, and re-layouts, place_frames(): return jnp.where(covered[:, None], incoming[source], text)  11.7 us
    all_to_all x1, starting transfers between devices, on_device(): lax.all_to_all(wide_place, ('seq', 'vis'), split_axis=0, concat_axis=0, t...  10.4 us
    all_to_all x1, starting transfers between devices, on_device(): lax.all_to_all(wide_rows, ('seq', 'vis'), split_axis=0, concat_axis=0, ti...  8.19 us
  transfers between devices with their start and end apart: 3, of which 3 were waited for; matrix products, arithmetic and copies ran while one was open for 7% of the time, Pallas kernels for 0%

commit v1 on v0

--- a/solution.py
+++ b/solution.py
@@ -119,7 +119,14 @@
             for entry in blocks
         )
     )
-    incoming_keys = lax.all_gather(keyval, "seq", axis=0, tiled=True)
+
+    def _unite_squares(x0, array_axis):
+        clean = lax.psum(1, "seq")
+        t1 = jnp.stack([x0] * clean)
+        built = lax.all_to_all(t1, axis_name="seq", split_axis=0, concat_axis=0)
+        return jnp.concatenate(built, axis=array_axis)
+
+    incoming_keys = _unite_squares(keyval, 0)
     piece_rows = incoming_keys.shape[0]
     step_rows = 512
 

time: 261 us -> 242 us (0.927)
  between operations: 14.4 us -> 1.05 us
  waiting for transfers between devices: 75.1 us -> 64.1 us
  starting transfers between devices: 18.6 us -> 26.8 us
    all_gather x1 -> x0, waiting for transfers between devices: 22.6 us -> none  [on_device(): incoming_keys = lax.all_gather(keyval, 'seq', axis=0, tiled=True)]
    all_to_all x0 -> x1, waiting for transfers between devices: none -> 11.5 us  [_unite_squares(): built = lax.all_to_all(t1, axis_name='seq', split_axis=0, concat_axis=0)]
    all_to_all x0 -> x1, starting transfers between devices: none -> 8.26 us  [_unite_squares(): built = lax.all_to_all(t1, axis_name='seq', split_axis=0, concat_axis=0)]
    while x1 -> x0, local copies, waits for them, and re-layouts: 4.09 us -> none  [on_device(): finals = lax.fori_loop(0, piece_rows // step_rows, one_step, initial)]
where the time goes in v1:
time: 242 us; the launch traced here: 241 us
  matrix products  74.8 us (31%)
  waiting for transfers between devices  64.1 us (26%)
  local copies, waits for them, and re-layouts  47.8 us (20%)
  starting transfers between devices  26.8 us (11%)
  other arithmetic  20 us (8%)
  loops' own time  5.92 us (2%)
    all_to_all x1, waiting for transfers between devices, on_device(): lax.all_to_all(wide_rows, ('seq', 'vis'), split_axis=0, concat_axis=0, ti...  48.9 us
    dot_general x8, matrix products, attend_block(): jnp.einsum('qgjd,kgd->qgjk', grouped, key_part, preferred_element_type=jn...  30.6 us
    dot_general x8, matrix products, attend_block(): jnp.einsum('qgjk,kgd->qgjd', raised.astype(jnp.bfloat16), value_part, pre...  28.5 us
    dot_general x1, matrix products, on_device(): jnp.dot(normed, w_query, preferred_element_type=jnp.float32) + q_bias  12.3 us
    gather x1, local copies, waits for them, and re-layouts, place_frames(): return jnp.where(covered[:, None], incoming[source], text)  11.7 us
    all_to_all x1, waiting for transfers between devices, _unite_squares(): built = lax.all_to_all(t1, axis_name='seq', split_axis=0, concat_axis=0)  11.5 us
    all_to_all x1, starting transfers between devices, on_device(): lax.all_to_all(wide_place, ('seq', 'vis'), split_axis=0, concat_axis=0, t...  10.4 us
    all_to_all x1, starting transfers between devices, _unite_squares(): built = lax.all_to_all(t1, axis_name='seq', split_axis=0, concat_axis=0)  8.26 us
  transfers between devices with their start and end apart: 3, of which 3 were waited for; matrix products, arithmetic and copies ran while one was open for 7% of the time, Pallas kernels for 0%

profile of v1, /device:TPU:57, one launch (start us, length us, event | category | flops | bytes accessed | tf_op | source)
XLA Modules:
  0.0 240.5 jit_solution(12456207047063107826)
XLA Ops:
  4.7 10.4 %all-to-all-start = ((s32[128,1,2]{2,1,0:T(1,128)}), s32[128,1,2]{2,1,0:T(1,128)S(1)}, u32[]{:S(2)}, u32[]{:S(2)}) async-start(s32[128,1,2]{2,1,0:T(1,128)} %bitcast.16), calls=%async_computation | async-start | bytes 131072 | tf_op jit(solution)/shard_map/all_to_all | solution.py:91
  22.1 6.1 %broadcast_in_dim.133 = bf16[16,8,2,8192]{3,2,1,0:T(2,128)(2,1)} broadcast(bf16[16,2,8192]{2,1,0:T(2,128)(2,1)S(1)} %broadcast_select_fusion.1), dimensions={0,2,3} | broadcast | bytes 4718592 | tf_op jit(solution)/shard_map/broadcast_in_dim | solution.py:85
  28.3 8.2 %all-to-all-start.1 = ((bf16[128,2,8192]{2,1,0:T(2,128)(2,1)}), bf16[128,2,8192]{2,1,0:T(2,128)(2,1)}, u32[]{:S(2)}, u32[]{:S(2)}) async-start(bf16[128,2,8192]{2,1,0:T(2,128)(2,1)} %bitcast.84), calls=%async_computation.1 | async-start | bytes 8388608 | tf_op jit(solution)/shard_map/all_to_all | solution.py:90
  37.1 48.9 %all-to-all-done.1 = bf16[128,2,8192]{2,1,0:T(2,128)(2,1)} async-done(((bf16[128,2,8192]{2,1,0:T(2,128)(2,1)}), bf16[128,2,8192]{2,1,0:T(2,128)(2,1)}, u32[]{:S(2)}, u32[]{:S(2)}) %all-to-all-start.1) | async-done | bytes 4194336 | tf_op jit(solution)/shard_map/all_to_all | solution.py:90
  86.0 7.2 %reshape.196 = bf16[256,8192]{1,0:T(8,128)(2,1)} reshape(bf16[128,2,8192]{2,1,0:T(2,128)(2,1)} %all-to-all-done.1) | data formatting | bytes 8388608 | tf_op jit(solution)/shard_map/reshape | solution.py:93
  93.2 11.7 %gather_fusion.2 = bf16[256,8192]{1,0:T(8,128)(2,1)} fusion(bf16[256,8192]{1,0:T(8,128)(2,1)} %reshape.196, s32[1024]{0:T(1024)S(1)} %pad_clamp_fusion), kind=kCustom, calls=%fused_computation.2 | custom fusion | bytes 8389632 | tf_op jit(solution)/shard_map/gather | solution.py:40
  104.8 5.1 %fusion.22 = f32[256]{0:T(256)S(1)} fusion(bf16[256,8192]{1,0:T(8,128)(2,1)} %gather_fusion.2, bf16[256,8192]{1,0:T(8,128)(2,1)} %param.15, pred[256]{0:T(512)(128)(4,1)S(1)} %fusion.28), kind=kLoop, calls=%fused_computation.31 | loop fusion | flops 8388352 | bytes 8389888 | tf_op jit(solution)/shard_map/reduce_sum | solution.py:97
  119.9 8.3 %all-to-all-start.2 = ((bf16[16,256,256]{2,1,0:T(8,128)(2,1)}), bf16[16,256,256]{2,1,0:T(8,128)(2,1)}, u32[]{:S(2)}, u32[]{:S(2)}) async-start(bf16[16,256,256]{2,1,0:T(8,128)(2,1)} %stack.2), calls=%async_computation.2 | async-start | bytes 4194304 | tf_op jit(solution)/shard_map/all_to_all | solution.py:126
  128.9 12.3 %fusion.25 = bf16[256,1024]{1,0:T(8,128)(2,1)} fusion(bf16[256,8192]{1,0:T(8,128)(2,1)} %copy-done.2, bf16[8192,1024]{1,0:T(8,128)(2,1)} %param.21, f32[1024]{0:T(1024)S(1)} %copy-done.8), kind=kOutput, calls=%fused_computation.36 | convolution fusion | flops 4295491584 | bytes 21499904 | tf_op jit(solution)/shard_map/dot_general | solution.py:99
  141.2 11.5 %all-to-all-done.2 = bf16[16,256,256]{2,1,0:T(8,128)(2,1)} async-done(((bf16[16,256,256]{2,1,0:T(8,128)(2,1)}), bf16[16,256,256]{2,1,0:T(8,128)(2,1)}, u32[]{:S(2)}, u32[]{:S(2)}) %all-to-all-start.2) | async-done | bytes 2097184 | tf_op jit(solution)/shard_map/all_to_all | solution.py:126
  152.9 84.8 %while.17 = (s32[]{:T(128)}, f32[256,1,8]{0,2,1:T(8,128)S(1)}, f32[256,1,8]{0,2,1:T(8,128)S(1)}, f32[256,1,8,128]{0,3,2,1:T(8,128)S(1)}, s32[256]{0:T(256)S(1)},...) while((s32[]{:T(128)}, f32[256,1,8]{0,2,1:T(8,128)S(1)}, ...), condition=%wide.region_11.12_spmd, body=%wide.region_6.11_spmd.sunk | while | flops 549329408 | bytes 32915828 | solution.py:162
  154.1 9.3 %conditional.2 = ((f32[256,1,8]{0,2,1:T(8,128)S(1)}, f32[256,1,8]{0,2,1:T(8,128)S(1)}, f32[256,1,8,128]{0,3,2,1:T(8,128)S(1)})) conditional(s32[]{:T(128)} %convert_element_type.65, (f32[256,1,8]{0,2,1:T(8,128)S(1)}, f32[256,1,8]{0,2,1:T(8,128)S(1)}, f32[256,1,8,128]{0,3,2,1:T(8,128)S(1)}) %tuple.48, (s32[]{:T(128)}, s32[512]{0:T(512)S(1)}, ...), branch_computations={%region_7.7_spmd, %region_8.10_spmd} | conditional | flops 549329408 | bytes 32913534 | solution.py:159
  155.1 3.8 %fusion = (f32[256,8]{0,1:T(8,128)S(1)}, f32[512,256,8]{1,0,2:T(8,128)}) fusion(pred[256,512]{0,1:T(8,128)(4,1)S(1)} %compare_and_fusion, bf16[4096,256]{1,0:T(8,128)(2,1)} %get-tuple-element.272, s32[]{:T(128)S(6)} %select_n.70, bf16[256,1024]{1,0:T(8,128)(2,1)} %get-tuple-element.273), kind=kOutput, calls=%fused_computation.5 | convolution fusion | flops 271579136 | bytes 4988932 | tf_op jit(solution)/shard_map/while/body/eval_jaxpr/cond/branch_1_fun/qgjd,kgd->qgjk/dot_general | solution.py:52
  164.7 9.3 %conditional.2 = ((f32[256,1,8]{0,2,1:T(8,128)S(1)}, f32[256,1,8]{0,2,1:T(8,128)S(1)}, f32[256,1,8,128]{0,3,2,1:T(8,128)S(1)})) conditional(s32[]{:T(128)} %convert_element_type.65, (f32[256,1,8]{0,2,1:T(8,128)S(1)}, f32[256,1,8]{0,2,1:T(8,128)S(1)}, f32[256,1,8,128]{0,3,2,1:T(8,128)S(1)}) %tuple.48, (s32[]{:T(128)}, s32[512]{0:T(512)S(1)}, ...), branch_computations={%region_7.7_spmd, %region_8.10_spmd} | conditional | flops 549329408 | bytes 32913534 | solution.py:159
  165.7 3.8 %fusion = (f32[256,8]{0,1:T(8,128)S(1)}, f32[512,256,8]{1,0,2:T(8,128)}) fusion(pred[256,512]{0,1:T(8,128)(4,1)S(1)} %compare_and_fusion, bf16[4096,256]{1,0:T(8,128)(2,1)} %get-tuple-element.272, s32[]{:T(128)S(6)} %select_n.70, bf16[256,1024]{1,0:T(8,128)(2,1)} %get-tuple-element.273), kind=kOutput, calls=%fused_computation.5 | convolution fusion | flops 271579136 | bytes 4988932 | tf_op jit(solution)/shard_map/while/body/eval_jaxpr/cond/branch_1_fun/qgjd,kgd->qgjk/dot_general | solution.py:52
  175.3 9.3 %conditional.2 = ((f32[256,1,8]{0,2,1:T(8,128)S(1)}, f32[256,1,8]{0,2,1:T(8,128)S(1)}, f32[256,1,8,128]{0,3,2,1:T(8,128)S(1)})) conditional(s32[]{:T(128)} %convert_element_type.65, (f32[256,1,8]{0,2,1:T(8,128)S(1)}, f32[256,1,8]{0,2,1:T(8,128)S(1)}, f32[256,1,8,128]{0,3,2,1:T(8,128)S(1)}) %tuple.48, (s32[]{:T(128)}, s32[512]{0:T(512)S(1)}, ...), branch_computations={%region_7.7_spmd, %region_8.10_spmd} | conditional | flops 549329408 | bytes 32913534 | solution.py:159
  176.3 3.8 %fusion = (f32[256,8]{0,1:T(8,128)S(1)}, f32[512,256,8]{1,0,2:T(8,128)}) fusion(pred[256,512]{0,1:T(8,128)(4,1)S(1)} %compare_and_fusion, bf16[4096,256]{1,0:T(8,128)(2,1)} %get-tuple-element.272, s32[]{:T(128)S(6)} %select_n.70, bf16[256,1024]{1,0:T(8,128)(2,1)} %get-tuple-element.273), kind=kOutput, calls=%fused_computation.5 | convolution fusion | flops 271579136 | bytes 4988932 | tf_op jit(solution)/shard_map/while/body/eval_jaxpr/cond/branch_1_fun/qgjd,kgd->qgjk/dot_general | solution.py:52
  185.9 9.3 %conditional.2 = ((f32[256,1,8]{0,2,1:T(8,128)S(1)}, f32[256,1,8]{0,2,1:T(8,128)S(1)}, f32[256,1,8,128]{0,3,2,1:T(8,128)S(1)})) conditional(s32[]{:T(128)} %convert_element_type.65, (f32[256,1,8]{0,2,1:T(8,128)S(1)}, f32[256,1,8]{0,2,1:T(8,128)S(1)}, f32[256,1,8,128]{0,3,2,1:T(8,128)S(1)}) %tuple.48, (s32[]{:T(128)}, s32[512]{0:T(512)S(1)}, ...), branch_computations={%region_7.7_spmd, %region_8.10_spmd} | conditional | flops 549329408 | bytes 32913534 | solution.py:159
  186.9 3.8 %fusion = (f32[256,8]{0,1:T(8,128)S(1)}, f32[512,256,8]{1,0,2:T(8,128)}) fusion(pred[256,512]{0,1:T(8,128)(4,1)S(1)} %compare_and_fusion, bf16[4096,256]{1,0:T(8,128)(2,1)} %get-tuple-element.272, s32[]{:T(128)S(6)} %select_n.70, bf16[256,1024]{1,0:T(8,128)(2,1)} %get-tuple-element.273), kind=kOutput, calls=%fused_computation.5 | convolution fusion | flops 271579136 | bytes 4988932 | tf_op jit(solution)/shard_map/while/body/eval_jaxpr/cond/branch_1_fun/qgjd,kgd->qgjk/dot_general | solution.py:52
  196.5 9.3 %conditional.2 = ((f32[256,1,8]{0,2,1:T(8,128)S(1)}, f32[256,1,8]{0,2,1:T(8,128)S(1)}, f32[256,1,8,128]{0,3,2,1:T(8,128)S(1)})) conditional(s32[]{:T(128)} %convert_element_type.65, (f32[256,1,8]{0,2,1:T(8,128)S(1)}, f32[256,1,8]{0,2,1:T(8,128)S(1)}, f32[256,1,8,128]{0,3,2,1:T(8,128)S(1)}) %tuple.48, (s32[]{:T(128)}, s32[512]{0:T(512)S(1)}, ...), branch_computations={%region_7.7_spmd, %region_8.10_spmd} | conditional | flops 549329408 | bytes 32913534 | solution.py:159
  197.5 3.8 %fusion = (f32[256,8]{0,1:T(8,128)S(1)}, f32[512,256,8]{1,0,2:T(8,128)}) fusion(pred[256,512]{0,1:T(8,128)(4,1)S(1)} %compare_and_fusion, bf16[4096,256]{1,0:T(8,128)(2,1)} %get-tuple-element.272, s32[]{:T(128)S(6)} %select_n.70, bf16[256,1024]{1,0:T(8,128)(2,1)} %get-tuple-element.273), kind=kOutput, calls=%fused_computation.5 | convolution fusion | flops 271579136 | bytes 4988932 | tf_op jit(solution)/shard_map/while/body/eval_jaxpr/cond/branch_1_fun/qgjd,kgd->qgjk/dot_general | solution.py:52
  207.1 9.3 %conditional.2 = ((f32[256,1,8]{0,2,1:T(8,128)S(1)}, f32[256,1,8]{0,2,1:T(8,128)S(1)}, f32[256,1,8,128]{0,3,2,1:T(8,128)S(1)})) conditional(s32[]{:T(128)} %convert_element_type.65, (f32[256,1,8]{0,2,1:T(8,128)S(1)}, f32[256,1,8]{0,2,1:T(8,128)S(1)}, f32[256,1,8,128]{0,3,2,1:T(8,128)S(1)}) %tuple.48, (s32[]{:T(128)}, s32[512]{0:T(512)S(1)}, ...), branch_computations={%region_7.7_spmd, %region_8.10_spmd} | conditional | flops 549329408 | bytes 32913534 | solution.py:159
  217.7 9.3 %conditional.2 = ((f32[256,1,8]{0,2,1:T(8,128)S(1)}, f32[256,1,8]{0,2,1:T(8,128)S(1)}, f32[256,1,8,128]{0,3,2,1:T(8,128)S(1)})) conditional(s32[]{:T(128)} %convert_element_type.65, (f32[256,1,8]{0,2,1:T(8,128)S(1)}, f32[256,1,8]{0,2,1:T(8,128)S(1)}, f32[256,1,8,128]{0,3,2,1:T(8,128)S(1)}) %tuple.48, (s32[]{:T(128)}, s32[512]{0:T(512)S(1)}, ...), branch_computations={%region_7.7_spmd, %region_8.10_spmd} | conditional | flops 549329408 | bytes 32913534 | solution.py:159
  228.3 9.3 %conditional.2 = ((f32[256,1,8]{0,2,1:T(8,128)S(1)}, f32[256,1,8]{0,2,1:T(8,128)S(1)}, f32[256,1,8,128]{0,3,2,1:T(8,128)S(1)})) conditional(s32[]{:T(128)} %convert_element_type.65, (f32[256,1,8]{0,2,1:T(8,128)S(1)}, f32[256,1,8]{0,2,1:T(8,128)S(1)}, f32[256,1,8,128]{0,3,2,1:T(8,128)S(1)}) %tuple.48, (s32[]{:T(128)}, s32[512]{0:T(512)S(1)}, ...), branch_computations={%region_7.7_spmd, %region_8.10_spmd} | conditional | flops 549329408 | bytes 32913534 | solution.py:159
  (152 shorter events, 84.8 us)
Async XLA Ops:
  0.0 113.5 %copy-start = (bf16[8192,128]{1,0:T(8,128)(2,1)S(1)}, bf16[8192,128]{1,0:T(8,128)(2,1)}, u32[]{:S(2)}) copy-start(bf16[8192,128]{1,0:T(8,128)(2,1)} %param.23) | copy-start | bytes 6291460
  4.7 17.4 %all-to-all-start = ((s32[128,1,2]{2,1,0:T(1,128)}), s32[128,1,2]{2,1,0:T(1,128)S(1)}, u32[]{:S(2)}, u32[]{:S(2)}) async-start(s32[128,1,2]{2,1,0:T(1,128)} %bitcast.16), calls=%async_computation | async-start | bytes 131072 | tf_op jit(solution)/shard_map/all_to_all | solution.py:91
  28.3 57.7 %all-to-all-start.1 = ((bf16[128,2,8192]{2,1,0:T(2,128)(2,1)}), bf16[128,2,8192]{2,1,0:T(2,128)(2,1)}, u32[]{:S(2)}, u32[]{:S(2)}) async-start(bf16[128,2,8192]{2,1,0:T(2,128)(2,1)} %bitcast.84), calls=%async_computation.1 | async-start | bytes 8388608 | tf_op jit(solution)/shard_map/all_to_all | solution.py:90
  93.2 16.8 %copy-start.6 = (f32[8192]{0:T(1024)S(1)}, f32[8192]{0:T(1024)}, u32[]{:S(2)}) copy-start(f32[8192]{0:T(1024)} %param.20) | copy-start | bytes 98308
  104.8 5.2 %copy-start.3 = (bf16[256,8192]{1,0:T(8,128)(2,1)S(1)}, bf16[256,8192]{1,0:T(8,128)(2,1)}, u32[]{:S(2)}) copy-start(bf16[256,8192]{1,0:T(8,128)(2,1)} %gather_fusion.2) | copy-start | bytes 12582916
  104.8 5.9 %copy-start.4 = (bf16[256,8192]{1,0:T(8,128)(2,1)S(1)}, bf16[256,8192]{1,0:T(8,128)(2,1)}, u32[]{:S(2)}) copy-start(bf16[256,8192]{1,0:T(8,128)(2,1)} %param.15) | copy-start | bytes 12582916
  113.5 4.7 %copy-start.2 = (bf16[256,8192]{1,0:T(8,128)(2,1)}, bf16[256,8192]{1,0:T(8,128)(2,1)S(1)}, u32[]{:S(2)}) copy-start(bf16[256,8192]{1,0:T(8,128)(2,1)S(1)} %fusion.24) | copy-start | bytes 12582916
  113.5 3.1 %copy-start.5 = (bf16[8192,128]{1,0:T(8,128)(2,1)S(1)}, bf16[8192,128]{1,0:T(8,128)(2,1)}, u32[]{:S(2)}) copy-start(bf16[8192,128]{1,0:T(8,128)(2,1)} %param.24) | copy-start | bytes 6291460
  113.5 3.1 %copy-start.7 = (f32[128]{0:T(128)S(1)}, f32[128]{0:T(128)}, u32[]{:S(2)}) copy-start(f32[128]{0:T(128)} %param.25) | copy-start | bytes 1540
  118.2 10.7 %copy-start.8 = (f32[1024]{0:T(1024)S(1)}, f32[1024]{0:T(1024)}, u32[]{:S(2)}) copy-start(f32[1024]{0:T(1024)} %param.22) | copy-start | bytes 12292
  119.9 32.9 %all-to-all-start.2 = ((bf16[16,256,256]{2,1,0:T(8,128)(2,1)}), bf16[16,256,256]{2,1,0:T(8,128)(2,1)}, u32[]{:S(2)}, u32[]{:S(2)}) async-start(bf16[16,256,256]{2,1,0:T(8,128)(2,1)} %stack.2), calls=%async_computation.2 | async-start | bytes 4194304 | tf_op jit(solution)/shard_map/all_to_all | solution.py:126
  159.0 3.6 %copy-start.1 = (f32[512,256,8]{1,0,2:T(8,128)S(1)}, f32[512,256,8]{1,0,2:T(8,128)}, u32[]{:S(2)}) copy-start(f32[512,256,8]{1,0,2:T(8,128)} %get-tuple-element.314) | copy-start | bytes 12582916 | tf_op jit(solution)/shard_map/while/body/eval_jaxpr/cond
  169.6 3.6 %copy-start.1 = (f32[512,256,8]{1,0,2:T(8,128)S(1)}, f32[512,256,8]{1,0,2:T(8,128)}, u32[]{:S(2)}) copy-start(f32[512,256,8]{1,0,2:T(8,128)} %get-tuple-element.314) | copy-start | bytes 12582916 | tf_op jit(solution)/shard_map/while/body/eval_jaxpr/cond
  180.2 3.6 %copy-start.1 = (f32[512,256,8]{1,0,2:T(8,128)S(1)}, f32[512,256,8]{1,0,2:T(8,128)}, u32[]{:S(2)}) copy-start(f32[512,256,8]{1,0,2:T(8,128)} %get-tuple-element.314) | copy-start | bytes 12582916 | tf_op jit(solution)/shard_map/while/body/eval_jaxpr/cond
  190.8 3.6 %copy-start.1 = (f32[512,256,8]{1,0,2:T(8,128)S(1)}, f32[512,256,8]{1,0,2:T(8,128)}, u32[]{:S(2)}) copy-start(f32[512,256,8]{1,0,2:T(8,128)} %get-tuple-element.314) | copy-start | bytes 12582916 | tf_op jit(solution)/shard_map/while/body/eval_jaxpr/cond
  201.4 3.6 %copy-start.1 = (f32[512,256,8]{1,0,2:T(8,128)S(1)}, f32[512,256,8]{1,0,2:T(8,128)}, u32[]{:S(2)}) copy-start(f32[512,256,8]{1,0,2:T(8,128)} %get-tuple-element.314) | copy-start | bytes 12582916 | tf_op jit(solution)/shard_map/while/body/eval_jaxpr/cond
  211.9 3.6 %copy-start.1 = (f32[512,256,8]{1,0,2:T(8,128)S(1)}, f32[512,256,8]{1,0,2:T(8,128)}, u32[]{:S(2)}) copy-start(f32[512,256,8]{1,0,2:T(8,128)} %get-tuple-element.314) | copy-start | bytes 12582916 | tf_op jit(solution)/shard_map/while/body/eval_jaxpr/cond
  222.5 3.6 %copy-start.1 = (f32[512,256,8]{1,0,2:T(8,128)S(1)}, f32[512,256,8]{1,0,2:T(8,128)}, u32[]{:S(2)}) copy-start(f32[512,256,8]{1,0,2:T(8,128)} %get-tuple-element.314) | copy-start | bytes 12582916 | tf_op jit(solution)/shard_map/while/body/eval_jaxpr/cond
  233.1 3.6 %copy-start.1 = (f32[512,256,8]{1,0,2:T(8,128)S(1)}, f32[512,256,8]{1,0,2:T(8,128)}, u32[]{:S(2)}) copy-start(f32[512,256,8]{1,0,2:T(8,128)} %get-tuple-element.314) | copy-start | bytes 12582916 | tf_op jit(solution)/shard_map/while/body/eval_jaxpr/cond
